TPU v7x, 512 devices: a whole 4x8x8 slice. The times are simulated.
512 devices in a mesh: site: 16 (over z, core), col: 32 (over x, y).
Axes of the slice: x: 4, y: 8, z: 8, core: 2. Of those that a mesh axis runs over, the one named last changes fastest.
Arguments:
- state_prev: float32 [128, 128, 8192], P('site', None, 'col'), may hold values from -6 to 6
- state_cur: float32 [128, 128, 8192], P('site', None, 'col'), may hold values from -6 to 6
- occupancy: int32 [4, 128, 128], replicated, may hold values 0 or 1
- panel_order: int32 [32], replicated, may hold values from 0 to 31, each once
Outputs:
- ortho_states: float32 [128, 128, 8192], P('site', None, 'col')
- growth: float32 [2, 256], replicated
Inputs may be any that keep to these rules, and one draw needn't show every extreme that they name: panel_order holds each panel number once.
All inputs are finite; a program needn't handle non-finite values.
Results may differ from a plain program's by a relative error of at most 0.000075.
Values sent between devices are 32-bit elements; how exact they have to be, the bound alone decides.
No kernel may reach another device: no remote copies, remote signals or barrier semaphores. Data moves between devices by JAX's collectives and lax.ppermute only.
A program may use at most 64 MiB of HBM per device.

v0:
```python
import jax
import jax.numpy as jnp
from jax import lax
from jax.sharding import PartitionSpec as P

STEPS = 4
PANEL = 256
ENERGY = 0.5
RESCALE = 0.015625


def from_root(value, axis, root):
    mine = lax.axis_index(axis) == root
    return lax.psum(jnp.where(mine, value, jnp.zeros_like(value)), axis)


def padded_2(value, sides, width):
    for axis, dim in sides:
        size, length = (lax.axis_size(axis), value.shape[dim])
        up = [(i, (i + 1) % size) for i in range(size)]
        down = [(j, i) for i, j in up]
        last = lax.slice_in_dim(value, length - width, length, axis=dim)
        leading = lax.slice_in_dim(value, 0, width, axis=dim)
        before = lax.ppermute(last, axis, up)
        after = lax.ppermute(leading, axis, down)
        value = jnp.concatenate([before, value, after], axis=dim)
    return value


def product(left, right):
    return jnp.dot(left, right, precision=lax.Precision.HIGHEST, preferred_element_type=jnp.float32)


def fetch_panel(flat, panel):
    count = PANEL // flat.shape[1]
    pieces = from_root(flat, "col", panel * count + 0)
    return pieces


def apply_inverse(lower, block):
    return jax.scipy.linalg.solve_triangular(lower, block.T, lower=True).T


def sweep_panel(flat, panel):
    block = fetch_panel(flat, panel)
    lower = jnp.linalg.cholesky(lax.psum(product(block.T, block), "site"))
    ortho = apply_inverse(lower, block)
    flat = flat - product(ortho, lax.psum(product(ortho.T, flat), "site"))
    return (flat, lower, ortho)


def place(result, ortho, panel, side):
    width = result.shape[1]
    offset = (lax.axis_index("col") - panel * (PANEL // width)) * width
    inside = jnp.logical_and(offset >= 0, offset < PANEL)
    return jnp.where(inside, ortho * float(side), result)


def on_device(state_prev, state_cur, occupancy, panel_order):
    rows, side, width = state_cur.shape
    start = lax.axis_index("site") * rows
    local_mask = lax.dynamic_slice_in_dim(occupancy, start, rows, 1)
    previous, current = (state_prev, state_cur)
    for turn in range(STEPS):
        weights = local_mask[turn].astype(jnp.float32)[:, :, None]
        padded = padded_2(current, (("site", 0),), 1)
        neighbours = padded[2:] + padded[:-2] + jnp.roll(current, 1, 1) + jnp.roll(current, -1, 1)
        previous, current = (current, weights * (ENERGY * current - neighbours - previous))
    flat = current.reshape(rows * side, width)
    first_panel = panel_order[0]
    second_panel = panel_order[1]
    flat, first_lower, first_q = sweep_panel(flat, first_panel)
    flat, second_lower, second_q = sweep_panel(flat, second_panel)
    result = flat * RESCALE
    result = place(result, first_q, first_panel, side)
    result = place(result, second_q, second_panel, side)
    growth = jnp.stack([jnp.log(jnp.diagonal(first_lower)), jnp.log(jnp.diagonal(second_lower))])
    return (result.reshape(rows, side, width), growth)


def solution(mesh):
    return jax.shard_map(
        on_device,
        mesh=mesh,
        in_specs=(P("site", None, "col"), P("site", None, "col"), P(), P()),
        out_specs=(P("site", None, "col"), P()),
        check_vma=False,
    )
```

profile of v0, /device:TPU:1, one launch (start us, length us, event | category | flops | bytes accessed | tf_op | source)
XLA Modules:
  0.0 974.7 jit_solution(11955733928134964861)
XLA Ops:
  7.2 1.0 fusion.76
  8.2 6.9 collective-permute-start
  15.1 0.9 fusion.75
  16.0 2.8 fusion.74
  18.8 0.6 fusion.77
  20.0 0.7 fusion.56
  20.8 1.9 fusion.26
  22.9 3.1 collective-permute-start.2
  26.1 1.3 collective-permute-done.2
  27.3 2.5 collective-permute-done.3
  30.5 4.8 collective-permute-start.4
  35.3 1.0 collective-permute-done.4
  36.2 1.0 collective-permute-done.5
  37.8 3.7 collective-permute-start.6
  41.5 1.4 collective-permute-done.6
  42.9 0.5 collective-permute-done.7
  44.3 0.6 copy-done.5
  44.9 1.1 broadcast_select_fusion.1
  46.1 155.3 %all-reduce.8.cloned.1.call-done = f32[1024,256]{0,1:T(8,128)} async-done(((f32[1024,256]{0,1:T(8,128)}), f32[1024,256]{0,1:T(8,128)}) %all-reduce.8.cloned.1.call-update) | async-done | bytes 1048592 | tf_op jit(solution)/shard_map/psum | solution.py:14
  201.3 3.3 fusion.78
  205.0 116.8 %all-reduce.10.cloned.1.call-done = f32[256,256]{0,1:T(8,128)} async-done(((f32[256,256]{0,1:T(8,128)}), f32[256,256]{0,1:T(8,128)}) %all-reduce.10.cloned.1.call-update) | async-done | bytes 262160 | tf_op jit(solution)/shard_map/psum | solution.py:46
  321.7 1.1 copy.16
  323.0 11.7 %cholesky.130 = f32[128,128]{1,0:T(8,128)S(1)} custom-call(f32[128,128]{1,0:T(8,128)S(1)} %cholesky.194), custom_call_target="Cholesky" | custom-call | tf_op jit(solution)/shard_map/jit(cholesky)/cholesky | solution.py:46
  334.7 9.8 %custom-call.17 = f32[1,128,128]{1,2,0:T(8,128)S(1)} custom-call(f32[1,128,128]{2,1,0:T(8,128)S(1)} %get-tuple-element.83), custom_call_target="InvertDiagBlocksLowerTriangular" | custom-call | tf_op jit(solution)/shard_map/jit(cholesky)/cholesky | solution.py:46
  345.0 11.7 %cholesky.147 = f32[128,128]{1,0:T(8,128)S(1)} custom-call(f32[128,128]{1,0:T(8,128)S(1)} %convolution_subtract_fusion.5), custom_call_target="Cholesky" | custom-call | tf_op jit(solution)/shard_map/jit(cholesky)/cholesky | solution.py:46
  356.8 0.7 compare_reduce_fusion.2
  358.9 4.6 while.4
  359.4 0.6 fusion.98
  360.1 1.3 bitcast_dynamic-update-slice_fusion.4
  361.5 0.6 fusion.98
  362.1 1.3 bitcast_dynamic-update-slice_fusion.4
  363.5 19.7 %custom-call.18 = f32[2,128,128]{1,2,0:T(8,128)S(1)} custom-call(f32[2,128,128]{2,1,0:T(8,128)S(1)} %get-tuple-element.18), custom_call_target="InvertDiagBlocksLowerTriangular" | custom-call | tf_op jit(solution)/shard_map/jit(_solve_triangular)/triangular_solve | solution.py:41
  383.2 0.6 fusion.31
  383.8 0.6 convolution_subtract_fusion.3
  384.4 0.6 fusion.44
  385.1 1.7 fusion.28
  387.5 113.8 %all-reduce.12.cloned.1.call-done = f32[256,256]{1,0:T(8,128)} async-done(((f32[256,256]{1,0:T(8,128)}), f32[256,256]{1,0:T(8,128)}) %all-reduce.12.cloned.1.call-update) | async-done | bytes 262160 | tf_op jit(solution)/shard_map/psum | solution.py:48
  501.3 3.4 broadcast_select_fusion
  504.7 156.2 %all-reduce.14.cloned.1.call-done = f32[1024,256]{0,1:T(8,128)} async-done(((f32[1024,256]{0,1:T(8,128)}), f32[1024,256]{0,1:T(8,128)}) %all-reduce.14.cloned.1.call-update) | async-done | bytes 1048592 | tf_op jit(solution)/shard_map/psum | solution.py:14
  660.9 3.3 fusion.79
  664.4 116.7 %all-reduce.16.cloned.1.call-done = f32[256,256]{0,1:T(8,128)} async-done(((f32[256,256]{0,1:T(8,128)}), f32[256,256]{0,1:T(8,128)}) %all-reduce.16.cloned.1.call-update) | async-done | bytes 262160 | tf_op jit(solution)/shard_map/psum | solution.py:46
  781.1 1.1 copy.19
  782.4 11.7 %cholesky.164 = f32[128,128]{1,0:T(8,128)S(1)} custom-call(f32[128,128]{1,0:T(8,128)S(1)} %cholesky.197), custom_call_target="Cholesky" | custom-call | tf_op jit(solution)/shard_map/jit(cholesky)/cholesky | solution.py:46
  794.1 0.6 compare_reduce_fusion.1
  794.8 9.8 %custom-call.19 = f32[1,128,128]{1,2,0:T(8,128)S(1)} custom-call(f32[1,128,128]{2,1,0:T(8,128)S(1)} %get-tuple-element.79), custom_call_target="InvertDiagBlocksLowerTriangular" | custom-call | tf_op jit(solution)/shard_map/jit(cholesky)/cholesky | solution.py:46
  805.1 11.7 %cholesky.181 = f32[128,128]{1,0:T(8,128)S(1)} custom-call(f32[128,128]{1,0:T(8,128)S(1)} %convolution_subtract_fusion.4), custom_call_target="Cholesky" | custom-call | tf_op jit(solution)/shard_map/jit(cholesky)/cholesky | solution.py:46
  816.8 0.7 compare_reduce_fusion
  818.9 0.7 fusion.38
  819.6 4.1 while.5
  819.9 0.6 fusion.99
  820.5 1.3 bitcast_dynamic-update-slice_fusion.5
  821.8 0.6 fusion.99
  822.4 1.3 bitcast_dynamic-update-slice_fusion.5
  823.7 19.7 %custom-call.20 = f32[2,128,128]{1,2,0:T(8,128)S(1)} custom-call(f32[2,128,128]{2,1,0:T(8,128)S(1)} %get-tuple-element.19), custom_call_target="InvertDiagBlocksLowerTriangular" | custom-call | tf_op jit(solution)/shard_map/jit(_solve_triangular)/triangular_solve | solution.py:41
  843.4 0.6 fusion.29
  844.1 0.6 convolution_subtract_fusion.2
  844.7 0.6 fusion.40
  845.3 1.7 fusion.27
  848.3 2.3 gather_fusion
  850.7 2.3 gather_fusion.1
  853.1 0.6 pad_maximum_fusion.14
  853.7 107.9 %all-reduce.18.cloned.1.call-done = f32[256,256]{1,0:T(8,128)} async-done(((f32[256,256]{1,0:T(8,128)}), f32[256,256]{1,0:T(8,128)}) %all-reduce.18.cloned.1.call-update) | async-done | bytes 262160 | tf_op jit(solution)/shard_map/psum | solution.py:48
  961.5 3.6 fusion.2
  965.1 2.5 copy.27
  (80 shorter events, 4.5 us)
Async XLA Ops:
  7.2 194.2 %all-reduce.8.cloned.1.call-start = ((), (), s32[]{:S(2)}) async-start(), calls=%async_computation | async-start | bytes 2097152 | tf_op jit(solution)/shard_map/psum | solution.py:14
  8.2 12.5 %collective-permute-start = (f32[1,128,256]{2,1,0:T(8,128)S(1)}, f32[1,128,256]{2,1,0:T(8,128)S(1)}, u32[]{:S(2)}, u32[]{:S(2)}) collective-permute-start(f32[1,128,256]{2,1,0:T(8,128)S(1)} %get-tuple-element.70), channel_id=1, source_target_pairs={{32,0},{64,32},{96,64},{128,96},{160,128},{192,160},{224,192},{256... | collective-permute-start | bytes 393224 | tf_op jit(solution)/shard_map/ppermute | solution.py:25
  15.1 5.7 collective-permute-start.1
  16.0 2.8 copy-start.11
  16.0 4.8 copy-start
  22.9 4.4 collective-permute-start.2
  26.0 3.8 collective-permute-start.3
  30.5 5.8 collective-permute-start.4
  35.3 2.0 collective-permute-start.5
  37.8 5.1 collective-permute-start.6
  41.5 2.0 collective-permute-start.7
  43.9 1.0 copy-start.5
  46.0 275.7 %all-reduce.10.cloned.1.call-start = ((), (), s32[]{:S(2)}) async-start(), calls=%async_computation.1 | async-start | bytes 524288 | tf_op jit(solution)/shard_map/psum | solution.py:46
  204.6 296.7 %all-reduce.12.cloned.1.call-start = ((), (), s32[]{:S(2)}) async-start(), calls=%async_computation.2 | async-start | bytes 524288 | tf_op jit(solution)/shard_map/psum | solution.py:48
  321.7 1.2 copy-start.9
  344.8 38.4 %copy-start.1 = (f32[1024,256]{0,1:T(8,128)S(1)}, f32[1024,256]{0,1:T(8,128)}, u32[]{:S(2)}) copy-start(f32[1024,256]{0,1:T(8,128)} %all-reduce.8.cloned.1.call-done) | copy-start | bytes 3145732
  383.8 1.2 copy-start.6
  386.8 274.1 %all-reduce.14.cloned.1.call-start = ((), (), s32[]{:S(2)}) async-start(), calls=%async_computation.3 | async-start | bytes 2097152 | tf_op jit(solution)/shard_map/psum | solution.py:14
  504.7 276.4 %all-reduce.16.cloned.1.call-start = ((), (), s32[]{:S(2)}) async-start(), calls=%async_computation.4 | async-start | bytes 524288 | tf_op jit(solution)/shard_map/psum | solution.py:46
  664.2 297.3 %all-reduce.18.cloned.1.call-start = ((), (), s32[]{:S(2)}) async-start(), calls=%async_computation.5 | async-start | bytes 524288 | tf_op jit(solution)/shard_map/psum | solution.py:48
  781.1 1.2 copy-start.10
  804.8 38.6 %copy-start.2 = (f32[1024,256]{0,1:T(8,128)S(1)}, f32[1024,256]{0,1:T(8,128)}, u32[]{:S(2)}) copy-start(f32[1024,256]{0,1:T(8,128)} %all-reduce.14.cloned.1.call-done) | copy-start | bytes 3145732
  844.1 1.3 copy-start.3
  845.3 1.8 copy-start.7
  848.3 2.4 copy-start.8
  848.3 113.2 %copy-start.4 = (f32[1024,256]{0,1:T(8,128)S(1)}, f32[1024,256]{0,1:T(8,128)}, u32[]{:S(2)}) copy-start(f32[1024,256]{0,1:T(8,128)} %get-tuple-element.89) | copy-start | bytes 3145732
Sparse Core Ops, SparseCore 0:
  46.1 155.1 all-reduce.7
  204.7 116.9 all-reduce.9
  386.9 114.3 all-reduce.11
  505.1 155.7 all-reduce.13
  664.3 116.7 all-reduce.15
  847.2 114.2 all-reduce.17
where the time goes:
time: 979 us; the launch traced here: 975 us
  waiting for transfers between devices  774 us (79%)
  other arithmetic  115 us (12%)
  local copies, waits for them, and re-layouts  24.4 us (2%)
  matrix products  21.6 us (2%)
  between operations  19.9 us (2%)
  starting transfers between devices  19.2 us (2%)
    psum x2, waiting for transfers between devices, from_root(): return lax.psum(jnp.where(mine, value, jnp.zeros_like(value)), axis)  311 us
    psum x2, waiting for transfers between devices, sweep_panel(): lower = jnp.linalg.cholesky(lax.psum(product(block.T, block), 'site'))  233 us
    psum x2, waiting for transfers between devices, sweep_panel(): flat = flat - product(ortho, lax.psum(product(ortho.T, flat), 'site'))  222 us
    another operation x13, other arithmetic, sweep_panel(): lower = jnp.linalg.cholesky(lax.psum(product(block.T, block), 'site'))  68.7 us
    another operation x5, other arithmetic, apply_inverse(): return jax.scipy.linalg.solve_triangular(lower, block.T, lower=True).T  40.1 us
  transfers between devices with their start and end apart: 14, of which 12 were waited for; matrix products, arithmetic and copies ran while one was open for 1% of the time, Pallas kernels for 0%

commit v1 on v0

--- a/solution.py
+++ b/solution.py
@@ -11,7 +11,7 @@
 
 def from_root(value, axis, root):
     mine = lax.axis_index(axis) == root
-    return lax.psum(jnp.where(mine, value, jnp.zeros_like(value)), axis)
+    return jnp.sum(lax.all_gather(jnp.where(mine, value, jnp.zeros_like(value)), axis), axis=0)
 
 
 def padded_2(value, sides, width):

time: 979 us -> 1190 us (1.22)
  waiting for transfers between devices: 774 us -> 928 us
  local copies, waits for them, and re-layouts: 24.4 us -> 54.1 us
  other arithmetic: 115 us -> 138 us
    all_gather x0 -> x2, waiting for transfers between devices: none -> 475 us  [from_root(): lax.all_gather(jnp.where(mine, value, jnp.zeros_like(value)), axis)]
    psum x2 -> x0, waiting for transfers between devices: 311 us -> none  [from_root(): return lax.psum(jnp.where(mine, value, jnp.zeros_like(value)), axis)]
    unnamed x25 -> x8, local copies, waits for them, and re-layouts: 3.21 us -> 32 us
    reduce_sum x0 -> x2, other arithmetic: none -> 19.4 us  [from_root(): jnp.sum(lax.all_gather(jnp.where(mine, value, jnp.zeros_like(value)), axi...]
where the time goes in v1:
time: 1190 us; the launch traced here: 1180 us
  waiting for transfers between devices  928 us (78%)
  other arithmetic  138 us (12%)
  local copies, waits for them, and re-layouts  54.1 us (5%)
  matrix products  23.4 us (2%)
  starting transfers between devices  19.7 us (2%)
  between operations  19.7 us (2%)
    all_gather x2, waiting for transfers between devices, from_root(): lax.all_gather(jnp.where(mine, value, jnp.zeros_like(value)), axis)  475 us
    psum x2, waiting for transfers between devices, sweep_panel(): lower = jnp.linalg.cholesky(lax.psum(product(block.T, block), 'site'))  224 us
    psum x2, waiting for transfers between devices, sweep_panel(): flat = flat - product(ortho, lax.psum(product(ortho.T, flat), 'site'))  221 us
    another operation x13, other arithmetic, sweep_panel(): lower = jnp.linalg.cholesky(lax.psum(product(block.T, block), 'site'))  68.6 us
    another operation x5, other arithmetic, apply_inverse(): return jax.scipy.linalg.solve_triangular(lower, block.T, lower=True).T  40.1 us
    unnamed x8, local copies, waits for them, and re-layouts  32 us
  transfers between devices with their start and end apart: 14, of which 12 were waited for; matrix products, arithmetic and copies ran while one was open for 1% of the time, Pallas kernels for 0%

profile of v1, /device:TPU:1, one launch (start us, length us, event | category | flops | bytes accessed | tf_op | source)
XLA Modules:
  0.0 1182.4 jit_solution(5662960657726558692)
XLA Ops:
  7.2 1.0 fusion.77
  8.2 6.9 collective-permute-start
  15.1 0.9 fusion.76
  16.0 1.8 fusion.75
  17.8 1.3 fusion.78
  19.7 0.7 fusion.56
  20.5 2.6 fusion.26
  23.3 3.3 collective-permute-start.2
  26.7 1.1 collective-permute-done.2
  27.7 2.5 collective-permute-done.3
  30.2 1.7 fusion.20
  32.1 4.8 collective-permute-start.4
  36.9 1.0 collective-permute-done.4
  37.9 1.0 collective-permute-done.5
  39.5 3.7 collective-permute-start.6
  43.2 1.4 collective-permute-done.6
  45.2 1.4 broadcast_select_fusion.1
  46.6 237.2 %all-gather.4.cloned.1.call-done = f32[32,1024,256]{2,1,0:T(8,128)} async-done(((f32[1,1024,256]{2,1,0:T(8,128)}), f32[32,1024,256]{2,1,0:T(8,128)}) %all-gather.4.cloned.1.call-update) | async-done | bytes 33554448 | tf_op jit(solution)/shard_map/all_gather | solution.py:14
  283.8 11.9 %reduce_sum.18 = f32[1024,256]{1,0:T(8,128)S(1)} reduce(f32[32,1024,256]{2,1,0:T(8,128)} %all-gather.4.cloned.1.call-done, f32[]{:T(128)} %constant.88.clone.1), dimensions={0}, to_apply=%region_0.1 | reduce | flops 8126464 | bytes 34603012 | tf_op jit(solution)/shard_map/reduce_sum | solution.py:14
  295.7 2.5 fusion.79
  298.9 1.3 copy.33
  300.2 110.9 %all-reduce.6.cloned.1.call-done = f32[256,256]{0,1:T(8,128)} async-done(((f32[256,256]{0,1:T(8,128)}), f32[256,256]{0,1:T(8,128)}) %all-reduce.6.cloned.1.call-update) | async-done | bytes 262160 | tf_op jit(solution)/shard_map/psum | solution.py:46
  411.1 1.1 copy.32
  412.2 1.0 fusion.34
  413.2 11.7 cholesky.130
  425.0 9.8 custom-call.17
  435.3 11.7 cholesky.147
  447.0 0.7 compare_reduce_fusion.2
  449.0 4.0 while.4
  449.8 1.3 bitcast_dynamic-update-slice_fusion.4
  451.7 1.3 bitcast_dynamic-update-slice_fusion.4
  453.0 19.7 %custom-call.18 = f32[2,128,128]{1,2,0:T(8,128)S(1)} custom-call(f32[2,128,128]{2,1,0:T(8,128)S(1)} %get-tuple-element.18), custom_call_target="InvertDiagBlocksLowerTriangular" | custom-call | tf_op jit(solution)/shard_map/jit(_solve_triangular)/triangular_solve | solution.py:41
  472.7 1.7 fusion.31
  474.4 1.6 convolution_subtract_fusion.3
  476.7 1.7 fusion.28
  479.4 113.4 %all-reduce.8.cloned.1.call-done = f32[256,256]{1,0:T(8,128)} async-done(((f32[256,256]{1,0:T(8,128)}), f32[256,256]{1,0:T(8,128)}) %all-reduce.8.cloned.1.call-update) | async-done | bytes 262160 | tf_op jit(solution)/shard_map/psum | solution.py:48
  592.9 3.0 broadcast_select_fusion
  596.0 238.1 %all-gather.6.cloned.1.call-done = f32[32768,256]{0,1:T(8,128)} async-done(((f32[1024,256]{0,1:T(8,128)}), f32[32768,256]{0,1:T(8,128)}) %all-gather.6.cloned.1.call-update) | async-done | bytes 33554448 | tf_op jit(solution)/shard_map/all_gather | solution.py:14
  834.1 28.8 %copy.45 = f32[32,8,32,1024]{3,2,1,0:T(8,128)S(1)} copy(f32[32,8,32,1024]{3,1,2,0:T(8,128)} %bitcast.99) | data formatting | bytes 67108864
  862.9 7.5 bitcast_reduce_fusion
  870.4 1.7 fusion.80
  872.4 112.6 %all-reduce.10.cloned.1.call-done = f32[256,256]{0,1:T(8,128)} async-done(((f32[256,256]{0,1:T(8,128)}), f32[256,256]{0,1:T(8,128)}) %all-reduce.10.cloned.1.call-update) | async-done | bytes 262160 | tf_op jit(solution)/shard_map/psum | solution.py:46
  985.0 1.1 copy.36
  986.1 1.0 fusion.33
  987.1 0.7 copy-done.2
  987.8 11.7 cholesky.164
  999.6 0.7 compare_reduce_fusion.1
  1000.2 9.8 custom-call.19
  1010.1 1.0 constant_dynamic-update-slice_fusion
  1011.1 1.1 convolution_subtract_fusion.4
  1012.2 11.7 cholesky.181
  1024.0 0.6 compare_reduce_fusion
  1025.9 0.7 fusion.38
  1026.7 4.1 while.5
  1027.5 1.3 bitcast_dynamic-update-slice_fusion.5
  1029.5 1.3 bitcast_dynamic-update-slice_fusion.5
  1030.7 19.7 %custom-call.20 = f32[2,128,128]{1,2,0:T(8,128)S(1)} custom-call(f32[2,128,128]{2,1,0:T(8,128)S(1)} %get-tuple-element.19), custom_call_target="InvertDiagBlocksLowerTriangular" | custom-call | tf_op jit(solution)/shard_map/jit(_solve_triangular)/triangular_solve | solution.py:41
  1051.1 1.4 convolution_subtract_fusion.2
  1053.1 1.7 fusion.27
  1056.2 2.3 gather_fusion
  1058.5 2.6 gather_fusion.1
  1061.7 107.7 %all-reduce.12.cloned.1.call-done = f32[256,256]{1,0:T(8,128)} async-done(((f32[256,256]{1,0:T(8,128)}), f32[256,256]{1,0:T(8,128)}) %all-reduce.12.cloned.1.call-update) | async-done | bytes 262160 | tf_op jit(solution)/shard_map/psum | solution.py:48
  1169.4 3.4 fusion.2
  1172.8 2.5 copy.44
  (65 shorter events, 8.8 us)
Async XLA Ops:
  7.2 276.7 %all-gather.4.cloned.1.call-start = ((), (), s32[]{:S(2)}) async-start(), calls=%async_computation | async-start | bytes 34603008 | tf_op jit(solution)/shard_map/all_gather | solution.py:14
  8.2 12.3 %collective-permute-start = (f32[1,128,256]{2,1,0:T(8,128)S(1)}, f32[1,128,256]{2,1,0:T(8,128)S(1)}, u32[]{:S(2)}, u32[]{:S(2)}) collective-permute-start(f32[1,128,256]{2,1,0:T(8,128)S(1)} %get-tuple-element.76), channel_id=1, source_target_pairs={{32,0},{64,32},{96,64},{128,96},{160,128},{192,160},{224,192},{256... | collective-permute-start | bytes 393224 | tf_op jit(solution)/shard_map/ppermute | solution.py:25
  15.1 5.4 collective-permute-start.1
  23.3 4.4 collective-permute-start.2
  26.6 3.6 collective-permute-start.3
  32.1 5.8 collective-permute-start.4
  36.9 2.0 collective-permute-start.5
  39.5 5.1 collective-permute-start.6
  43.2 2.0 collective-permute-start.7
  46.5 364.6 %all-reduce.6.cloned.1.call-start = ((), (), s32[]{:S(2)}) async-start(), calls=%async_computation.1 | async-start | bytes 524288 | tf_op jit(solution)/shard_map/psum | solution.py:46
  298.3 294.6 %all-reduce.8.cloned.1.call-start = ((), (), s32[]{:S(2)}) async-start(), calls=%async_computation.2 | async-start | bytes 524288 | tf_op jit(solution)/shard_map/psum | solution.py:48
  476.6 357.5 %copy-start = (f32[128,1024]{1,0:T(8,128)}, f32[128,1024]{1,0:T(8,128)S(1)}, u32[]{:S(2)}) copy-start(f32[128,1024]{1,0:T(8,128)S(1)} %fusion.44) | copy-start | bytes 1572868
  478.4 355.7 %all-gather.6.cloned.1.call-start = ((), (), s32[]{:S(2)}) async-start(), calls=%async_computation.5 | async-start | bytes 34603008 | tf_op jit(solution)/shard_map/all_gather | solution.py:14
  595.9 389.1 %all-reduce.10.cloned.1.call-start = ((), (), s32[]{:S(2)}) async-start(), calls=%async_computation.3 | async-start | bytes 524288 | tf_op jit(solution)/shard_map/psum | solution.py:46
  872.1 297.2 %all-reduce.12.cloned.1.call-start = ((), (), s32[]{:S(2)}) async-start(), calls=%async_computation.4 | async-start | bytes 524288 | tf_op jit(solution)/shard_map/psum | solution.py:48
  987.1 0.7 copy-start.2
  1030.7 19.7 %copy-start.1 = (f32[256,256]{1,0:T(8,128)}, f32[256,256]{1,0:T(8,128)S(1)}, u32[]{:S(2)}) copy-start(f32[256,256]{1,0:T(8,128)S(1)} %get-tuple-element.200) | copy-start | bytes 786436
Sparse Core Ops, SparseCore 0:
  46.7 237.0 all-gather.3
  298.4 112.6 all-reduce.5
  478.5 114.2 all-reduce.7
  596.5 237.6 all-gather.5
  872.3 112.7 all-reduce.9
  1055.0 114.3 all-reduce.11
